TPU v7x, 128 devices: a whole 4x4x4 slice. The times are simulated.
128 devices in a mesh: copy: 2 (over x_hi), ctx: 32 (over y, z, x_lo), tp: 2 (over core).
Axes of the slice: x: 4 (x_hi: 2, x_lo: 2; x = x_hi * 2 + x_lo), y: 4, z: 4, core: 2. Of those that a mesh axis runs over, the one named last changes fastest.
Arguments:
- clean_tokens: bfloat16 [8192, 4096], P('ctx', 'copy'), may hold values from -36 to 36
- norm_gain: bfloat16 [4096], replicated, may hold values from 0.5 to 1.5
- mask_embed: bfloat16 [4096], replicated, may hold values from -6 to 6
- time_shift: float32 [4096], replicated, may hold values from -0.5 to 0.5
- w_query: bfloat16 [4096, 2048], P(None, 'tp'), may hold values from -0.09375 to 0.09375
- w_key: bfloat16 [4096, 512], P(None, 'tp'), may hold values from -0.09375 to 0.09375
- w_value: bfloat16 [4096, 512], P(None, 'tp'), may hold values from -0.09375 to 0.09375
- w_out: bfloat16 [2048, 4096], P('tp'), may hold values from -0.125 to 0.125
- q_gain: float32 [128], replicated, may hold values from 2 to 3
- k_gain: float32 [128], replicated, may hold values from 0.5 to 1.5
- masked: int32 [2, 8192], P('copy', 'ctx'), may hold values 0 or 1
- block_live: int32 [2, 128], P('copy', 'ctx'), may hold values 0 or 1
- timesteps: int32 [2], P('copy'), may hold values from 1 to 1000
Outputs:
- clean_out: bfloat16 [8192, 4096], P('ctx', 'tp')
- noised_out: bfloat16 [2, 8192, 4096], P('copy', 'ctx', 'tp')
All inputs are finite; a program needn't handle non-finite values. No bound on the sum of `masked` or of `block_live` on one device may be relied on, other than what follows from the above.
Results may differ from a plain program's by a relative error of at most 0.012.
The roundings to bfloat16 on the way count: a program that leaves them out, or rounds other values in their place, can miss the bound.
Values may be sent and summed in bfloat16 or wider, within the bound.
A program may use at most 320 MiB of HBM per device.

v0:
```python
import math
import jax
import jax.numpy as jnp
from jax import lax
from jax.sharding import PartitionSpec as P

HD = 128
BLK = 64
TSTEPS = 1000
EPS = 1e-06


def inverse_rms(values):
    return lax.rsqrt(jnp.mean(values * values, axis=-1, keepdims=True) + EPS)


def key_terms(state, queries, query_start, key_piece, value_piece, key_start):
    numerator, denominator = state
    streams_count, row_count, kv_local, group_size, head_dim = queries.shape
    piece_rows = key_piece.shape[0]
    key_heads = key_piece.reshape(piece_rows, kv_local, head_dim)
    value_heads = value_piece.reshape(piece_rows, kv_local, head_dim)

    def compute():
        scores = jnp.einsum(
            "srhgd,khd->srhgk", queries, key_heads, preferred_element_type=jnp.float32
        ) * (1.0 / math.sqrt(head_dim))
        query_blocks = (query_start + jnp.arange(row_count, dtype=jnp.int32)) // BLK
        key_blocks = jnp.arange(piece_rows, dtype=jnp.int32) // BLK
        offset = jnp.minimum(jnp.arange(streams_count, dtype=jnp.int32), 1)
        allowed = key_blocks[None, None, :] + offset[:, None, None] <= query_blocks[None, :, None]
        weights = jnp.where(allowed[:, :, None, None, :], jnp.exp(scores), 0.0)
        updated = jnp.einsum(
            "srhgk,khd->srhgd",
            weights.astype(jnp.bfloat16),
            value_heads,
            preferred_element_type=jnp.float32,
        )
        return (updated, jnp.sum(weights, axis=4))

    def unchanged():
        return (numerator, denominator)

    needed = key_start // BLK <= (query_start + row_count - 1) // BLK
    return lax.cond(needed, compute, unchanged)


def own_block(queries, key_heads, value_heads):
    copies, row_count, kv_local, group_size, head_dim = queries.shape
    count_blocks = row_count // BLK
    query_blocks = queries.reshape(copies, count_blocks, BLK, kv_local, group_size, head_dim)
    key_blocks = key_heads.reshape(copies, count_blocks, BLK, kv_local, head_dim)
    value_blocks = value_heads.reshape(copies, count_blocks, BLK, kv_local, head_dim)
    scores = jnp.einsum(
        "cbqhgd,cbkhd->cbqhgk", query_blocks, key_blocks, preferred_element_type=jnp.float32
    ) * (1.0 / math.sqrt(head_dim))
    weights = jnp.exp(scores)
    numerator = jnp.einsum(
        "cbqhgk,cbkhd->cbqhgd",
        weights.astype(jnp.bfloat16),
        value_blocks,
        preferred_element_type=jnp.float32,
    )
    denominator = jnp.sum(weights, axis=5)
    return (
        numerator.reshape(copies, row_count, kv_local, group_size, head_dim),
        denominator.reshape(copies, row_count, kv_local, group_size),
    )


def on_device(
    clean_tokens,
    norm_gain,
    mask_embed,
    time_shift,
    w_query,
    w_key,
    w_value,
    w_out,
    q_gain,
    k_gain,
    masked,
    block_live,
    timesteps,
):
    features = lax.all_gather(clean_tokens, "copy", axis=1, tiled=True)
    local_rows = features.shape[0]
    width = features.shape[1]
    copies = masked.shape[0]
    streams_count = 1 + copies
    kv_local = w_key.shape[1] // HD
    heads_local = w_query.shape[1] // HD
    group_size = heads_local // kv_local
    features_wide = features.astype(jnp.float32)
    gain_wide = norm_gain.astype(jnp.float32)
    normed_clean = (features_wide * inverse_rms(features_wide) * gain_wide).astype(jnp.bfloat16)
    noisy_tokens = jnp.where(
        masked[:, :, None] == 1, mask_embed[None, None, :], features[None, :, :]
    )
    noisy_wide = noisy_tokens.astype(jnp.float32)
    condition = (
        1.0 + timesteps.astype(jnp.float32)[:, None, None] / TSTEPS * time_shift[None, None, :]
    )
    normed_noisy = (noisy_wide * inverse_rms(noisy_wide) * gain_wide * condition).astype(
        jnp.bfloat16
    )
    all_rows = jnp.concatenate([normed_clean[None], normed_noisy], axis=0).reshape(-1, width)
    query_wide = jnp.dot(all_rows, w_query, preferred_element_type=jnp.float32).reshape(
        streams_count, local_rows, kv_local, group_size, HD
    )
    queries = (query_wide * inverse_rms(query_wide) * q_gain).astype(jnp.bfloat16)
    key_wide = jnp.dot(all_rows, w_key, preferred_element_type=jnp.float32).reshape(
        streams_count, local_rows, kv_local, HD
    )
    key_heads = (key_wide * inverse_rms(key_wide) * k_gain).astype(jnp.bfloat16)
    value_heads = (
        jnp.dot(all_rows, w_value, preferred_element_type=jnp.float32)
        .astype(jnp.bfloat16)
        .reshape(streams_count, local_rows, kv_local, HD)
    )
    clean_keys = key_heads[0].reshape(local_rows, kv_local * HD)
    clean_values = value_heads[0].reshape(local_rows, kv_local * HD)
    position = lax.axis_index("ctx")
    first_row = position * local_rows
    groups = ((queries, first_row, key_heads[1:], value_heads[1:]),)
    initial = tuple(
        (
            (jnp.zeros(member[0].shape, jnp.float32), jnp.zeros(member[0].shape[:-1], jnp.float32))
            for member in groups
        )
    )
    piece = (
        lax.all_gather(clean_keys, "ctx", axis=0, tiled=True),
        lax.all_gather(clean_values, "ctx", axis=0, tiled=True),
    )
    key_start = jnp.int32(0)
    totals = tuple(
        (
            key_terms(
                initial[number], groups[number][0], groups[number][1], piece[0], piece[1], key_start
            )
            for number in range(len(groups))
        )
    )
    number = 0
    numerator, denominator = totals[number]
    member = groups[number]
    self_numerator, own_den = own_block(member[0][1:], member[2], member[3])
    numerator = jnp.concatenate([numerator[:1], numerator[1:] + self_numerator], axis=0)
    denominator = jnp.concatenate([denominator[:1], denominator[1:] + own_den], axis=0)
    results = (numerator / denominator[..., None]).astype(jnp.bfloat16)
    head_rows = results.reshape(streams_count * local_rows, heads_local * HD)
    mixed = lax.psum_scatter(
        jnp.dot(head_rows, w_out, preferred_element_type=jnp.float32),
        "tp",
        scatter_dimension=1,
        tiled=True,
    )
    clean_out = mixed[:local_rows].astype(jnp.bfloat16)
    live_rows = jnp.repeat(block_live, BLK, axis=1).astype(jnp.float32)
    noised_out = (
        mixed[local_rows:].reshape(copies, local_rows, -1) * live_rows[:, :, None]
    ).astype(jnp.bfloat16)
    return (clean_out, noised_out)


def solution(mesh):
    in_specs = (
        P("ctx", "copy"),
        P(),
        P(),
        P(),
        P(None, "tp"),
        P(None, "tp"),
        P(None, "tp"),
        P("tp", None),
        P(),
        P(),
        P("copy", "ctx"),
        P("copy", "ctx"),
        P("copy"),
    )
    out_specs = (P("ctx", "tp"), P("copy", "ctx", "tp"))
    return jax.shard_map(
        on_device, mesh=mesh, in_specs=in_specs, out_specs=out_specs, check_vma=False
    )
```

profile of v0, /device:TPU:1, one launch (start us, length us, event | category | flops | bytes accessed | tf_op | source)
XLA Modules:
  0.0 565.8 jit_solution(7580052467397267353)
XLA Ops:
  7.2 0.0 copy-start
  7.2 0.0 copy-start.12
  7.2 0.0 copy-start.9
  7.2 0.0 copy-start.8
  7.2 0.0 all-gather.4.cloned.1.call-start
  7.3 0.7 all-gather.4.cloned.1.call-update
  7.9 0.0 all-gather.6.cloned.1.call-start
  8.6 0.7 convert_element_type.72
  9.3 4.1 copy.93
  13.5 0.0 copy-done.12
  13.5 0.0 copy-done.9
  13.5 36.6 %all-gather.4.cloned.1.call-done = bf16[256,4096]{1,0:T(8,128)(2,1)} async-done(((bf16[256,2048]{1,0:T(8,128)(2,1)}), bf16[256,4096]{1,0:T(8,128)(2,1)}) %all-gather.4.cloned.1.call-update) | async-done | bytes 2097168 | tf_op jit(solution)/shard_map/all_gather | solution.py:86
  50.1 0.0 copy-done.8
  50.1 3.4 fusion.19
  53.5 4.2 fusion.31
  57.7 0.0 copy-start.2
  57.7 0.0 copy-start.4
  57.7 0.0 copy-done.7
  57.7 0.0 copy-start.10
  57.7 1.3 multiply_reduce_fusion.1
  59.0 0.6 copy-done.4
  59.7 0.1 multiply_convert_fusion.1
  59.8 0.7 copy.66
  60.6 0.0 all-gather.6.cloned.1.call-update
  60.6 0.0 all-gather.8.cloned.1.call-start
  60.7 2.6 pad_maximum_fusion
  63.3 1.3 convolution_convert_fusion
  64.6 0.7 fusion.43
  65.2 0.0 all-gather.8.cloned.1.call-update
  65.3 0.0 reduce-scatter.2.cloned.1.call-start
  65.3 0.0 copy-start.3
  65.3 11.4 %copy.94 = bf16[1024,4096]{1,0:T(8,128)(2,1)} copy(bf16[1024,4096]{0,1:T(8,128)(2,1)} %bitcast.72) | data formatting | bytes 16777216 | tf_op jit(solution)/shard_map/dot_general | solution.py:108
  76.7 0.1 copy.71
  76.9 0.0 copy-start.11
  76.9 8.2 %multiply_reduce_fusion = (f32[2,256,2,4]{1,3,2,0:T(4,128)S(1)}, f32[2,256,2,4,128]{4,1,3,2,0:T(8,128)S(1)}) fusion(bf16[2,4,128,4096,1]{3,2,1,0,4:T(8,128)(2,1)} %bitcast.73, bf16[1,256,4096]{2,1,0:T(8,128)(2,1)} %copy-done.4, bf16[1,256,4096]{2,1,0:T(8,128)(2,1)S(1)} %copy-done.3), kind=kOutput, calls=%fused_computation.50 | convolution fusion | flops 4304400384 | bytes 14696448 | tf_op jit(solution)/shard_map/dot_general | solution.py:108
  85.1 0.7 multiply_convert_fusion
  85.8 0.0 copy-start.5
  85.9 0.7 fusion.46
  86.5 0.1 reshape.232
  86.6 0.1 copy-done.5
  86.8 0.3 convolution_bitcast_fusion
  87.1 0.1 copy.76
  87.2 118.4 %all-gather.6.cloned.1.call-done = bf16[8192,256]{1,0:T(8,128)(2,1)} async-done(((bf16[256,256]{1,0:T(8,128)(2,1)}), bf16[8192,256]{1,0:T(8,128)(2,1)}) %all-gather.6.cloned.1.call-update) | async-done | bytes 4194320 | tf_op jit(solution)/shard_map/all_gather | solution.py:133
  205.6 168.3 %all-gather.8.cloned.1.call-done = bf16[8192,256]{1,0:T(8,128)(2,1)} async-done(((bf16[256,256]{1,0:T(8,128)(2,1)}), bf16[8192,256]{1,0:T(8,128)(2,1)}) %all-gather.8.cloned.1.call-update) | async-done | bytes 4194320 | tf_op jit(solution)/shard_map/all_gather | solution.py:134
  373.9 126.5 %conditional.1 = (f32[2,256,2,4,128]{4,1,3,0,2:T(8,128)S(1)}, f32[2,256,2,4]{1,3,0,2:T(4,128)S(1)}) conditional(s32[]{:T(128)} %convert_element_type.70, () %tuple.16, (s32[]{:T(128)}, bf16[8192,256]{1,0:T(8,128)(2,1)}, bf16[2,256,2,4,128]{4,1,3,2,0:T(8,128)(2,1)}, bf16[8192,256]{1,0:T(8,128)(2,1)}) %tuple.45), branch_computations={%region_4.5_spmd, %region_5.7_spmd} | conditional | flops 17385472000 | bytes 313739328 | solution.py:45
  374.0 0.1 broadcast_add_fusion
  374.1 7.8 %broadcast_compare_fusion = pred[2,256,8192]{1,2,0:T(8,128)(4,1)} fusion(s32[256]{0:T(256)S(1)} %and_select_fusion, s32[2,8192]{1,0:T(2,128)S(1)} %broadcast_add_fusion), kind=kLoop, calls=%fused_computation.5 | loop fusion | flops 4194304 | bytes 4260864 | tf_op jit(solution)/shard_map/cond/branch_1_fun/le | solution.py:31
  381.9 7.0 %reshape.217 = bf16[8192,2,128]{2,1,0:T(2,128)(2,1)} reshape(bf16[8192,256]{1,0:T(8,128)(2,1)} %get-tuple-element.11) | data formatting | bytes 8388608 | tf_op jit(solution)/shard_map/reshape | solution.py:21
  388.9 48.1 %fusion = (f32[2,256,2,4]{1,3,0,2:T(4,128)S(1)}, f32[2,8192,2,256,4]{3,1,4,2,0:T(8,128)}) fusion(pred[2,256,8192]{1,2,0:T(8,128)(4,1)} %broadcast_compare_fusion, bf16[2,256,2,4,128]{4,1,3,2,0:T(8,128)(2,1)S(1)} %copy-done.6, bf16[8192,2,128,1,1]{2,1,0,4,3:T(2,128)(2,1)} %bitcast.74), kind=kOutput, calls=%fused_computation.1 | convolution fusion | flops 8690593792 | bytes 143671296 | tf_op jit(solution)/shard_map/cond/branch_1_fun/srhgd,khd->srhgk/dot_general | solution.py:25
  437.0 6.9 %reshape.218 = bf16[8192,2,128]{2,1,0:T(2,128)(2,1)} reshape(bf16[8192,256]{1,0:T(8,128)(2,1)} %get-tuple-element.13) | data formatting | bytes 8388608 | tf_op jit(solution)/shard_map/reshape | solution.py:22
  443.9 56.5 %fusion.8 = f32[2,256,2,4,128]{4,1,3,0,2:T(8,128)S(1)} fusion(bf16[8192,2,128,1,1]{2,1,0,4,3:T(2,128)(2,1)} %bitcast.75, f32[2,8192,2,256,4]{3,1,4,2,0:T(8,128)} %get-tuple-element.39, pred[2,256,8192]{1,2,0:T(8,128)(4,1)} %broadcast_compare_fusion), kind=kOutput, calls=%fused_computation.9 | convolution fusion | flops 8690597888 | bytes 144703488 | tf_op jit(solution)/shard_map/cond/branch_1_fun/srhgk,khd->srhgd/dot_general | solution.py:33
  500.4 0.2 fusion.42
  500.6 0.7 fusion.33
  501.4 0.8 copy.80
  502.2 0.8 convert_element_type.83
  503.0 10.0 %fusion.47 = f32[512,4096]{1,0:T(8,128)} fusion(bf16[512,1024]{1,0:T(8,128)(2,1)S(1)} %convert_element_type.83, bf16[1024,4096]{1,0:T(8,128)(2,1)} %param.22), kind=kOutput, calls=%fused_computation.80 | convolution fusion | flops 4294967296 | bytes 17825792 | tf_op jit(solution)/shard_map/dot_general | solution.py:154
  513.0 0.0 reduce-scatter.2.cloned.1.call-update
  513.0 0.6 copy-done.13
  513.7 0.1 broadcast_in_dim.37
  513.7 0.1 convert_element_type.86
  513.8 40.0 %reduce-scatter.2.cloned.1.call-done = f32[512,2048]{1,0:T(8,128)} async-done(((f32[512,4096]{1,0:T(8,128)}), f32[512,2048]{1,0:T(8,128)}) %reduce-scatter.2.cloned.1.call-update) | async-done | bytes 4194320 | tf_op jit(solution)/shard_map/reduce_scatter | solution.py:153
  553.8 2.7 slice.66
  556.5 2.7 fusion.36
  559.3 0.0 copy-done.1
  (25 shorter events, 0.2 us)
Async XLA Ops:
  7.2 56.1 %copy-start = (bf16[4096,256]{1,0:T(8,128)(2,1)S(1)}, bf16[4096,256]{1,0:T(8,128)(2,1)}, u32[]{:S(2)}) copy-start(bf16[4096,256]{1,0:T(8,128)(2,1)} %param.21) | copy-start | bytes 6291460
  7.2 6.3 %copy-start.12 = (s32[1,256]{1,0:T(1,128)S(1)}, s32[1,256]{1,0:T(1,128)}, u32[]{:S(2)}) copy-start(s32[1,256]{1,0:T(1,128)} %param.25) | copy-start | bytes 3076
  7.2 6.3 %copy-start.9 = (f32[4096]{0:T(1024)S(1)}, f32[4096]{0:T(1024)}, u32[]{:S(2)}) copy-start(f32[4096]{0:T(1024)} %param.18) | copy-start | bytes 49156
  7.2 42.9 %copy-start.8 = (bf16[4096]{0:T(1024)(128)(2,1)S(1)}, bf16[4096]{0:T(1024)(128)(2,1)}, u32[]{:S(2)}) copy-start(bf16[4096]{0:T(1024)(128)(2,1)} %param.17) | copy-start | bytes 24580
  7.2 42.9 %all-gather.4.cloned.1.call-start = ((), (), s32[]{:S(2)}) async-start(), calls=%async_computation.1 | async-start | bytes 3145728 | tf_op jit(solution)/shard_map/all_gather | solution.py:86
  7.9 197.7 %all-gather.6.cloned.1.call-start = ((), (), s32[]{:S(2)}) async-start(), calls=%async_computation.2 | async-start | bytes 4325376 | tf_op jit(solution)/shard_map/all_gather | solution.py:133
  50.1 7.6 %copy-start.7 = (bf16[256,4096]{1,0:T(8,128)(2,1)S(1)}, bf16[256,4096]{1,0:T(8,128)(2,1)}, u32[]{:S(2)}) copy-start(bf16[256,4096]{1,0:T(8,128)(2,1)} %copy.93) | copy-start | bytes 6291460
  57.7 1.4 copy-start.2
  57.7 2.0 copy-start.4
  57.7 2.0 copy-start.10
  60.6 313.3 %all-gather.8.cloned.1.call-start = ((), (), s32[]{:S(2)}) async-start(), calls=%async_computation.3 | async-start | bytes 4325376 | tf_op jit(solution)/shard_map/all_gather | solution.py:134
  65.3 488.6 %reduce-scatter.2.cloned.1.call-start = ((), (), s32[]{:S(2)}) async-start(), calls=%async_computation.4 | async-start | bytes 12582912 | tf_op jit(solution)/shard_map/reduce_scatter | solution.py:153
  65.3 11.5 %copy-start.3 = (bf16[1,256,4096]{2,1,0:T(8,128)(2,1)S(1)}, bf16[1,256,4096]{2,1,0:T(8,128)(2,1)}, u32[]{:S(2)}) copy-start(bf16[1,256,4096]{2,1,0:T(8,128)(2,1)} %copy-done.2) | copy-start | bytes 6291460
  76.9 8.2 %copy-start.11 = (f32[128]{0:T(128)S(1)}, f32[128]{0:T(128)}, u32[]{:S(2)}) copy-start(f32[128]{0:T(128)} %param.23) | copy-start | bytes 1540
  85.8 1.0 copy-start.5
  381.9 7.0 %copy-start.6 = (bf16[2,256,2,4,128]{4,1,3,2,0:T(8,128)(2,1)S(1)}, bf16[2,256,2,4,128]{4,1,3,2,0:T(8,128)(2,1)}, u32[]{:S(2)}) copy-start(bf16[2,256,2,4,128]{4,1,3,2,0:T(8,128)(2,1)} %get-tuple-element.34) | copy-start | bytes 3145732 | tf_op jit(solution)/shard_map/cond
  513.0 0.7 copy-start.13
  513.7 45.6 %copy-start.1 = (bf16[4096,256]{1,0:T(8,128)(2,1)S(1)}, bf16[4096,256]{1,0:T(8,128)(2,1)}, u32[]{:S(2)}) copy-start(bf16[4096,256]{1,0:T(8,128)(2,1)} %param.21) | copy-start | bytes 6291460
Sparse Core Ops, SparseCore 0:
  9.7 40.3 all-gather.3
  60.7 144.8 all-gather.5
  207.8 166.0 all-gather.7
  513.2 40.6 reduce-scatter.1
where the time goes:
time: 567 us; the launch traced here: 566 us
  waiting for transfers between devices  364 us (64%)
  matrix products  126 us (22%)
  local copies, waits for them, and re-layouts  37.2 us (7%)
  other arithmetic  23.4 us (4%)
  between operations  14.7 us (3%)
    all_gather x1, waiting for transfers between devices, on_device(): lax.all_gather(clean_values, 'ctx', axis=0, tiled=True)  168 us
    all_gather x1, waiting for transfers between devices, on_device(): lax.all_gather(clean_keys, 'ctx', axis=0, tiled=True)  118 us
    dot_general x1, matrix products, compute(): jnp.einsum('srhgk,khd->srhgd', weights.astype(jnp.bfloat16), value_heads,...  56.5 us
    dot_general x1, matrix products, compute(): jnp.einsum('srhgd,khd->srhgk', queries, key_heads, preferred_element_type...  48.1 us
    reduce_scatter x1, waiting for transfers between devices, on_device(): lax.psum_scatter(jnp.dot(head_rows, w_out, preferred_element_type=jnp.flo...  40 us
    all_gather x1, waiting for transfers between devices, on_device(): features = lax.all_gather(clean_tokens, 'copy', axis=1, tiled=True)  36.6 us
    dot_general x1, local copies, waits for them, and re-layouts, on_device(): jnp.dot(all_rows, w_query, preferred_element_type=jnp.float32)  11.4 us
  transfers between devices with their start and end apart: 4, of which 4 were waited for; matrix products, arithmetic and copies ran while one was open for 6% of the time, Pallas kernels for 0%

commit v1 on v0

--- a/solution.py
+++ b/solution.py
@@ -131,7 +131,9 @@
     )
     piece = (
         lax.all_gather(clean_keys, "ctx", axis=0, tiled=True),
-        lax.all_gather(clean_values, "ctx", axis=0, tiled=True),
+        jnp.concatenate(
+            lax.all_to_all(jnp.stack([clean_values] * lax.axis_size("ctx")), "ctx", 0, 0), axis=0
+        ),
     )
     key_start = jnp.int32(0)
     totals = tuple(

time: 567 us -> 427 us (0.75)
  waiting for transfers between devices: 364 us -> 215 us
  starting transfers between devices: 0.16 us -> 7.24 us
    all_gather x1 -> x0, waiting for transfers between devices: 168 us -> none  [on_device(): lax.all_gather(clean_values, 'ctx', axis=0, tiled=True)]
    all_to_all x0 -> x1, waiting for transfers between devices: none -> 83.8 us  [on_device(): lax.all_to_all(jnp.stack([clean_values] * lax.axis_size('ctx')), 'ctx', 0...]
    all_gather x1, waiting for transfers between devices: 118 us -> 58.7 us  [on_device(): lax.all_gather(clean_keys, 'ctx', axis=0, tiled=True)]
    another operation x1 -> x3, local copies, waits for them, and re-layouts: 0.04 us -> 9.41 us  [the longest x1 6.94 us: key_terms(): value_heads = value_piece.reshape(piece_rows, kv_local, head_dim)]
    all_to_all x0 -> x1, starting transfers between devices: none -> 7.12 us  [on_device(): lax.all_to_all(jnp.stack([clean_values] * lax.axis_size('ctx')), 'ctx', 0...]
    reshape x1 -> x0, local copies, waits for them, and re-layouts: 6.93 us -> none  [key_terms(): value_heads = value_piece.reshape(piece_rows, kv_local, head_dim)]
  transfers between devices with their start and end apart: 4 -> 4, of which waited for: 4 -> 4; matrix products, arithmetic and copies ran while one was open for 6% -> 8% of each run, Pallas kernels for 0% -> 0%
where the time goes in v1:
time: 427 us; the launch traced here: 426 us
  waiting for transfers between devices  215 us (50%)
  matrix products  126 us (30%)
  local copies, waits for them, and re-layouts  39.1 us (9%)
  other arithmetic  23.4 us (5%)
  between operations  14.7 us (3%)
  starting transfers between devices  7.24 us (2%)
    all_to_all x1, waiting for transfers between devices, on_device(): lax.all_to_all(jnp.stack([clean_values] * lax.axis_size('ctx')), 'ctx', 0...  83.8 us
    all_gather x1, waiting for transfers between devices, on_device(): lax.all_gather(clean_keys, 'ctx', axis=0, tiled=True)  58.7 us
    dot_general x1, matrix products, compute(): jnp.einsum('srhgk,khd->srhgd', weights.astype(jnp.bfloat16), value_heads,...  56.5 us
    dot_general x1, matrix products, compute(): jnp.einsum('srhgd,khd->srhgk', queries, key_heads, preferred_element_type...  48.1 us
    all_gather x1, waiting for transfers between devices, on_device(): features = lax.all_gather(clean_tokens, 'copy', axis=1, tiled=True)  36.6 us
    reduce_scatter x1, waiting for transfers between devices, on_device(): lax.psum_scatter(jnp.dot(head_rows, w_out, preferred_element_type=jnp.flo...  35.1 us
    dot_general x1, local copies, waits for them, and re-layouts, on_device(): jnp.dot(all_rows, w_query, preferred_element_type=jnp.float32)  11.6 us
    dot_general x1, matrix products, on_device(): jnp.dot(head_rows, w_out, preferred_element_type=jnp.float32)  10.1 us
  transfers between devices with their start and end apart: 4, of which 4 were waited for; matrix products, arithmetic and copies ran while one was open for 8% of the time, Pallas kernels for 0%

profile of v1, /device:TPU:1, one launch (start us, length us, event | category | flops | bytes accessed | tf_op | source)
XLA Modules:
  0.0 425.8 jit_solution(3484438408404583273)
XLA Ops:
  7.2 0.0 copy-start
  7.2 0.0 copy-start.12
  7.2 0.0 copy-start.9
  7.2 0.0 copy-start.8
  7.2 0.0 all-gather.3.cloned.1.call-start
  7.3 0.7 all-gather.3.cloned.1.call-update
  7.9 0.0 all-gather.5.cloned.1.call-start
  8.6 0.7 convert_element_type.72
  9.3 4.1 copy.93
  13.5 0.0 copy-done.12
  13.5 0.0 copy-done.9
  13.5 36.6 %all-gather.3.cloned.1.call-done = bf16[256,4096]{1,0:T(8,128)(2,1)} async-done(((bf16[256,2048]{1,0:T(8,128)(2,1)}), bf16[256,4096]{1,0:T(8,128)(2,1)}) %all-gather.3.cloned.1.call-update) | async-done | bytes 2097168 | tf_op jit(solution)/shard_map/all_gather | solution.py:86
  50.1 0.0 copy-done.8
  50.1 3.4 fusion.19
  53.5 4.2 fusion.31
  57.7 0.0 copy-start.2
  57.7 0.0 copy-start.4
  57.7 0.0 copy-done.7
  57.7 0.0 copy-start.10
  57.7 1.3 multiply_reduce_fusion.1
  59.0 0.0 copy-done.2
  59.0 0.6 copy-done.4
  59.7 0.0 copy-done.10
  59.7 0.1 multiply_convert_fusion.1
  59.8 0.8 copy.66
  60.6 0.0 all-gather.5.cloned.1.call-update
  60.6 2.6 pad_maximum_fusion
  63.2 1.3 convolution_convert_fusion
  64.5 2.4 stack.3
  67.0 7.1 %all-to-all-start = ((bf16[32,256,256]{2,1,0:T(8,128)(2,1)}), bf16[32,256,256]{2,1,0:T(8,128)(2,1)}, u32[]{:S(2)}, u32[]{:S(2)}) async-start(bf16[32,256,256]{2,1,0:T(8,128)(2,1)} %stack.3), calls=%async_computation | async-start | bytes 8388608 | tf_op jit(solution)/shard_map/all_to_all | solution.py:135
  74.1 0.0 reduce-scatter.2.cloned.1.call-start
  74.2 11.6 %copy.94 = bf16[1024,4096]{1,0:T(8,128)(2,1)} copy(bf16[1024,4096]{0,1:T(8,128)(2,1)} %bitcast.72) | data formatting | bytes 16777216 | tf_op jit(solution)/shard_map/dot_general | solution.py:108
  85.7 0.1 copy.71
  85.9 0.0 copy-start.11
  85.9 8.1 %multiply_reduce_fusion = (f32[2,256,2,4]{1,3,2,0:T(4,128)S(1)}, f32[2,256,2,4,128]{4,1,3,2,0:T(8,128)S(1)}) fusion(bf16[2,4,128,4096,1]{3,2,1,0,4:T(8,128)(2,1)} %bitcast.73, bf16[1,256,4096]{2,1,0:T(8,128)(2,1)} %copy-done.4, bf16[1,256,4096]{2,1,0:T(8,128)(2,1)S(1)} %copy-done.3), kind=kOutput, calls=%fused_computation.50 | convolution fusion | flops 4304400384 | bytes 14696448 | tf_op jit(solution)/shard_map/dot_general | solution.py:108
  94.0 0.7 multiply_convert_fusion
  94.8 0.0 copy-start.5
  94.8 0.7 fusion.46
  95.5 0.1 reshape.230
  95.6 0.1 copy-done.5
  95.7 0.3 convolution_bitcast_fusion
  96.1 0.1 copy.76
  96.2 83.8 %all-to-all-done = bf16[32,256,256]{2,1,0:T(8,128)(2,1)} async-done(((bf16[32,256,256]{2,1,0:T(8,128)(2,1)}), bf16[32,256,256]{2,1,0:T(8,128)(2,1)}, u32[]{:S(2)}, u32[]{:S(2)}) %all-to-all-start) | async-done | bytes 4194336 | tf_op jit(solution)/shard_map/all_to_all | solution.py:135
  180.0 58.7 %all-gather.5.cloned.1.call-done = bf16[8192,256]{1,0:T(8,128)(2,1)} async-done(((bf16[256,256]{1,0:T(8,128)(2,1)}), bf16[8192,256]{1,0:T(8,128)(2,1)}) %all-gather.5.cloned.1.call-update) | async-done | bytes 4194320 | tf_op jit(solution)/shard_map/all_gather | solution.py:133
  238.7 126.6 %conditional.1 = (f32[2,256,2,4,128]{4,1,3,0,2:T(8,128)S(1)}, f32[2,256,2,4]{1,3,0,2:T(4,128)S(1)}) conditional(s32[]{:T(128)} %convert_element_type.70, () %tuple.16, (s32[]{:T(128)}, bf16[8192,256]{1,0:T(8,128)(2,1)}, bf16[2,256,2,4,128]{4,1,3,2,0:T(8,128)(2,1)}, bf16[32,256,256]{2,1,0:T(8,128)(2,1)}) %tuple.43), branch_computations={%region_4.5_spmd, %region_5.7_spmd} | conditional | flops 17385472000 | bytes 313739328 | solution.py:45
  238.7 0.1 broadcast_add_fusion
  238.8 7.9 %broadcast_compare_fusion = pred[2,256,8192]{1,2,0:T(8,128)(4,1)} fusion(s32[256]{0:T(256)S(1)} %and_select_fusion, s32[2,8192]{1,0:T(2,128)S(1)} %broadcast_add_fusion), kind=kLoop, calls=%fused_computation.5 | loop fusion | flops 4194304 | bytes 4260864 | tf_op jit(solution)/shard_map/cond/branch_1_fun/le | solution.py:31
  246.7 7.0 %reshape.216 = bf16[8192,2,128]{2,1,0:T(2,128)(2,1)} reshape(bf16[8192,256]{1,0:T(8,128)(2,1)} %get-tuple-element.11) | data formatting | bytes 8388608 | tf_op jit(solution)/shard_map/reshape | solution.py:21
  253.7 0.0 copy-done.6
  253.7 48.1 %fusion = (f32[2,256,2,4]{1,3,0,2:T(4,128)S(1)}, f32[2,8192,2,256,4]{3,1,4,2,0:T(8,128)}) fusion(pred[2,256,8192]{1,2,0:T(8,128)(4,1)} %broadcast_compare_fusion, bf16[2,256,2,4,128]{4,1,3,2,0:T(8,128)(2,1)S(1)} %copy-done.6, bf16[8192,2,128,1,1]{2,1,0,4,3:T(2,128)(2,1)} %bitcast.74), kind=kOutput, calls=%fused_computation.1 | convolution fusion | flops 8690593792 | bytes 143671296 | tf_op jit(solution)/shard_map/cond/branch_1_fun/srhgd,khd->srhgk/dot_general | solution.py:25
  301.8 6.9 %reshape_reshape.3 = bf16[8192,2,128]{2,1,0:T(2,128)(2,1)} reshape(bf16[32,256,256]{2,1,0:T(8,128)(2,1)} %get-tuple-element.13) | data formatting | bytes 8388608 | tf_op jit(solution)/shard_map/reshape;reshape | solution.py:22
  308.7 56.5 %fusion.8 = f32[2,256,2,4,128]{4,1,3,0,2:T(8,128)S(1)} fusion(bf16[8192,2,128,1,1]{2,1,0,4,3:T(2,128)(2,1)} %bitcast.75, f32[2,8192,2,256,4]{3,1,4,2,0:T(8,128)} %get-tuple-element.39, pred[2,256,8192]{1,2,0:T(8,128)(4,1)} %broadcast_compare_fusion), kind=kOutput, calls=%fused_computation.9 | convolution fusion | flops 8690597888 | bytes 144703488 | tf_op jit(solution)/shard_map/cond/branch_1_fun/srhgk,khd->srhgd/dot_general | solution.py:33
  365.3 0.2 fusion.42
  365.5 0.7 fusion.33
  366.2 0.8 copy.80
  367.0 0.8 convert_element_type.83
  367.8 10.1 %fusion.47 = f32[512,4096]{1,0:T(8,128)} fusion(bf16[512,1024]{1,0:T(8,128)(2,1)S(1)} %convert_element_type.83, bf16[1024,4096]{1,0:T(8,128)(2,1)} %param.22), kind=kOutput, calls=%fused_computation.80 | convolution fusion | flops 4294967296 | bytes 17825792 | tf_op jit(solution)/shard_map/dot_general | solution.py:156
  377.8 0.0 reduce-scatter.2.cloned.1.call-update
  377.9 0.6 copy-done.13
  378.5 0.1 broadcast_in_dim.37
  378.6 0.1 convert_element_type.86
  378.7 35.1 %reduce-scatter.2.cloned.1.call-done = f32[512,2048]{1,0:T(8,128)} async-done(((f32[512,4096]{1,0:T(8,128)}), f32[512,2048]{1,0:T(8,128)}) %reduce-scatter.2.cloned.1.call-update) | async-done | bytes 4194320 | tf_op jit(solution)/shard_map/reduce_scatter | solution.py:155
  413.8 2.7 slice.66
  416.5 2.7 fusion.36
  (25 shorter events, 0.2 us)
Async XLA Ops:
  7.2 56.1 %copy-start = (bf16[4096,256]{1,0:T(8,128)(2,1)S(1)}, bf16[4096,256]{1,0:T(8,128)(2,1)}, u32[]{:S(2)}) copy-start(bf16[4096,256]{1,0:T(8,128)(2,1)} %param.21) | copy-start | bytes 6291460
  7.2 6.3 %copy-start.12 = (s32[1,256]{1,0:T(1,128)S(1)}, s32[1,256]{1,0:T(1,128)}, u32[]{:S(2)}) copy-start(s32[1,256]{1,0:T(1,128)} %param.25) | copy-start | bytes 3076
  7.2 6.3 %copy-start.9 = (f32[4096]{0:T(1024)S(1)}, f32[4096]{0:T(1024)}, u32[]{:S(2)}) copy-start(f32[4096]{0:T(1024)} %param.18) | copy-start | bytes 49156
  7.2 42.9 %copy-start.8 = (bf16[4096]{0:T(1024)(128)(2,1)S(1)}, bf16[4096]{0:T(1024)(128)(2,1)}, u32[]{:S(2)}) copy-start(bf16[4096]{0:T(1024)(128)(2,1)} %param.17) | copy-start | bytes 24580
  7.2 42.9 %all-gather.3.cloned.1.call-start = ((), (), s32[]{:S(2)}) async-start(), calls=%async_computation.2 | async-start | bytes 3145728 | tf_op jit(solution)/shard_map/all_gather | solution.py:86
  7.9 230.7 %all-gather.5.cloned.1.call-start = ((), (), s32[]{:S(2)}) async-start(), calls=%async_computation.3 | async-start | bytes 4325376 | tf_op jit(solution)/shard_map/all_gather | solution.py:133
  50.1 7.6 %copy-start.7 = (bf16[256,4096]{1,0:T(8,128)(2,1)S(1)}, bf16[256,4096]{1,0:T(8,128)(2,1)}, u32[]{:S(2)}) copy-start(bf16[256,4096]{1,0:T(8,128)(2,1)} %copy.93) | copy-start | bytes 6291460
  57.7 1.4 copy-start.2
  57.7 2.0 copy-start.4
  57.7 2.0 copy-start.10
  67.0 113.0 %all-to-all-start = ((bf16[32,256,256]{2,1,0:T(8,128)(2,1)}), bf16[32,256,256]{2,1,0:T(8,128)(2,1)}, u32[]{:S(2)}, u32[]{:S(2)}) async-start(bf16[32,256,256]{2,1,0:T(8,128)(2,1)} %stack.3), calls=%async_computation | async-start | bytes 8388608 | tf_op jit(solution)/shard_map/all_to_all | solution.py:135
  74.1 339.7 %reduce-scatter.2.cloned.1.call-start = ((), (), s32[]{:S(2)}) async-start(), calls=%async_computation.4 | async-start | bytes 12582912 | tf_op jit(solution)/shard_map/reduce_scatter | solution.py:155
  74.2 11.7 %copy-start.3 = (bf16[1,256,4096]{2,1,0:T(8,128)(2,1)S(1)}, bf16[1,256,4096]{2,1,0:T(8,128)(2,1)}, u32[]{:S(2)}) copy-start(bf16[1,256,4096]{2,1,0:T(8,128)(2,1)} %copy-done.2) | copy-start | bytes 6291460
  85.9 8.2 %copy-start.11 = (f32[128]{0:T(128)S(1)}, f32[128]{0:T(128)}, u32[]{:S(2)}) copy-start(f32[128]{0:T(128)} %param.23) | copy-start | bytes 1540
  94.8 1.0 copy-start.5
  246.7 7.0 %copy-start.6 = (bf16[2,256,2,4,128]{4,1,3,2,0:T(8,128)(2,1)S(1)}, bf16[2,256,2,4,128]{4,1,3,2,0:T(8,128)(2,1)}, u32[]{:S(2)}) copy-start(bf16[2,256,2,4,128]{4,1,3,2,0:T(8,128)(2,1)} %get-tuple-element.34) | copy-start | bytes 3145732 | tf_op jit(solution)/shard_map/cond
  377.8 0.7 copy-start.13
  378.5 40.7 %copy-start.1 = (bf16[4096,256]{1,0:T(8,128)(2,1)S(1)}, bf16[4096,256]{1,0:T(8,128)(2,1)}, u32[]{:S(2)}) copy-start(bf16[4096,256]{1,0:T(8,128)(2,1)} %param.21) | copy-start | bytes 6291460
Sparse Core Ops, SparseCore 0:
  9.7 40.3 all-gather.2
  60.7 177.8 all-gather.4
  378.0 35.7 reduce-scatter.1
